TPU v7x, 256 devices: a whole 4x4x8 slice. The times are simulated.
256 devices in a mesh: dp: 4 (over y), mp: 16 (over x, z_lo), section: 4 (over z_hi, core).
Axes of the slice: x: 4, y: 4, z: 8 (z_hi: 2, z_lo: 4; z = z_hi * 4 + z_lo), core: 2. Of those that a mesh axis runs over, the one named last changes fastest.
Arguments:
- hidden_in: bfloat16 [64, 2560], P('dp', 'mp'), may hold values from -6 to 6
- lengths: int32 [64], P('dp'), may hold values from 0 to 7
- slots: int32 [64], P('dp'), may hold values from 0 to 71, as said below
- norm_gain: float32 [4, 2560], P('section'), may hold values from 0.5 to 1.5
- w_zxo: bfloat16 [4, 3, 5120, 2560], P('section', None, 'dp', 'mp'), may hold values from -0.125 to 0.125
- w_bcdt: bfloat16 [4, 336, 2560], P('section', 'dp', 'mp'), may hold values from -0.125 to 0.125
- conv_x_weight: float32 [4, 4, 5120], P('section', None, 'mp'), may hold values from -0.5 to 0.5
- conv_bc_weight: float32 [4, 4, 256], P('section'), may hold values from -0.5 to 0.5
- conv_x_pool: bfloat16 [4, 72, 3, 5120], P('section', 'dp', None, 'mp'), may hold values from -6 to 6
- conv_bc_pool: bfloat16 [4, 72, 3, 256], P('section', 'dp'), may hold values from -6 to 6
- state_pool: float32 [4, 72, 80, 64, 128], P('section', 'dp', 'mp'), may hold values from -1 to 1
- a_rate: float32 [4, 80], P('section', 'mp'), may hold values from 1 to 16
- dt_bias: float32 [4, 80], P('section', 'mp'), may hold values from -3 to 0
- skip_gain: float32 [4, 80], P('section', 'mp'), may hold values from 0.5 to 1.5
- gate_gain: float32 [4, 5120], P('section', 'mp'), may hold values from 0.5 to 1.5
Outputs:
- hidden_out: bfloat16 [4, 64, 2560], P('section', 'dp', 'mp')
- state_out: float32 [4, 64, 80, 64, 128], P('section', 'dp', 'mp')
Inputs may be any that keep to these rules, and one draw needn't show every extreme that they name: The sequences of the d-th block of 16 name distinct slots, all from d * 18 to (d + 1) * 18 - 1.
All inputs are finite; a program needn't handle non-finite values.
Results may differ from a plain program's by a relative error of at most 0.025.
Values may be sent and summed in bfloat16 or wider, within the bound.
A program may use at most 128 MiB of HBM per device.

v0:
```python
import jax
import jax.numpy as jnp
from jax import lax
from jax.sharding import PartitionSpec as P

MICRO = 4
epsilon = 1e-05


def copy_for_each(array, axis):
    devices = lax.axis_size(axis)
    return lax.all_to_all(
        jnp.broadcast_to(array[None], (devices, *array.shape)), axis, 0, 0, tiled=True
    )


def joined_along(tiles, dim):
    tiles = jnp.moveaxis(tiles, 0, dim)
    lengths = tiles.shape
    return tiles.reshape(*lengths[:dim], lengths[dim] * lengths[dim + 1], *lengths[dim + 2 :])


def gathered_copies(array, axis, dim):
    tiles = copy_for_each(array, axis)
    return joined_along(tiles, dim)


def over_copies(array, axis):
    return copy_for_each(array, axis).sum(axis=0)


def over_copies_2(array, axis):
    return copy_for_each(array, axis).astype(jnp.float32).sum(axis=0)


def passed_along(array, axis, by):
    devices = lax.axis_size(axis)
    pairs = [(i, i + by) for i in range(devices) if 0 <= i + by < devices]
    return lax.ppermute(array, axis, pairs)


def project(inputs, weights):
    return lax.dot_general(
        inputs, weights, (((1,), (1,)), ((), ())), preferred_element_type=jnp.float32
    )


def convolve(history, current, kernel, tap_mask):
    past_sum = jnp.sum(
        history.astype(jnp.float32) * tap_mask[:, :, None] * kernel[None, :3, :], axis=1
    )
    return jax.nn.silu(past_sum + current * kernel[3][None, :])


def local(
    hidden_in,
    lengths,
    slots,
    norm_gain,
    w_zxo,
    w_bcdt,
    conv_x_weight,
    conv_bc_weight,
    conv_x_pool,
    conv_bc_pool,
    state_pool,
    a_rate,
    dt_bias,
    skip_gain,
    gate_gain,
):
    section_index = lax.axis_index("section")
    section_count = lax.axis_size("section")
    mp_index = lax.axis_index("mp")
    mp_count = lax.axis_size("mp")
    dp_index = lax.axis_index("dp")
    seq_dev = hidden_in.shape[0]
    micro_rows = seq_dev // MICRO
    model_width = norm_gain.shape[1]
    model_share = hidden_in.shape[1]
    heads_dev = a_rate.shape[1]
    head_size = state_pool.shape[3]
    state_size = state_pool.shape[4]
    chan_dev = heads_dev * head_size
    slots_dev = state_pool.shape[1]
    bc_width = conv_bc_weight.shape[2]
    half_width = bc_width // 2
    zxo_rows, small_rows = (
        lax.all_gather(w_zxo, "dp", axis=2, tiled=True),
        lax.all_gather(w_bcdt[:, None], "dp", axis=2, tiled=True),
    )
    proj_weights = lax.all_to_all(zxo_rows, "mp", split_axis=2, concat_axis=3, tiled=True)[0]
    small_full = gathered_copies(small_rows, "mp", 3)[0, 0]
    entry_full = gathered_copies(hidden_in, "mp", 1)
    pre_gain = norm_gain[0]
    post_gain = gate_gain[0]
    kernel_x = conv_x_weight[0]
    kernel_bc = conv_bc_weight[0]
    rate_heads = a_rate[0]
    bias_heads = dt_bias[0]
    skip_heads = skip_gain[0]
    local_slots = slots - dp_index * slots_dev
    tick_count = MICRO + section_count - 1
    hidden_buffer = jnp.zeros((seq_dev, model_share), jnp.bfloat16)
    state_buffer = jnp.zeros((seq_dev, heads_dev, head_size, state_size), jnp.float32)
    received = None
    for tick_index in range(tick_count):
        if tick_index < MICRO:
            first_rows = entry_full[tick_index * micro_rows : (tick_index + 1) * micro_rows]
        else:
            first_rows = jnp.zeros((micro_rows, model_width), jnp.bfloat16)
        if tick_index == 0:
            layer_input = first_rows
        else:
            layer_input = jnp.where(section_index == 0, first_rows, received)
        micro_index = tick_index - section_index
        in_range = (micro_index >= 0) & (micro_index < MICRO)
        row_start = jnp.clip(micro_index, 0, MICRO - 1) * micro_rows
        rows_length = lax.dynamic_slice_in_dim(lengths, row_start, micro_rows)
        rows_slot = lax.dynamic_slice_in_dim(local_slots, row_start, micro_rows)
        tap_mask = (rows_length[:, None] >= (3 - jnp.arange(3, dtype=jnp.int32))[None, :]).astype(
            jnp.float32
        )
        alive = (rows_length > 0).astype(jnp.float32)
        residual = layer_input.astype(jnp.float32)
        normed_in = (
            residual
            * lax.rsqrt(jnp.mean(residual * residual, axis=1, keepdims=True) + epsilon)
            * pre_gain[None, :]
        ).astype(jnp.bfloat16)
        gate_proj = project(normed_in, proj_weights[0])
        inner_proj = project(normed_in, proj_weights[1])
        small_proj = project(normed_in, small_full)
        step_raw = lax.dynamic_slice_in_dim(
            small_proj, bc_width + mp_index * heads_dev, heads_dev, 1
        )
        conv_x = convolve(
            jnp.take(conv_x_pool[0], rows_slot, axis=0), inner_proj, kernel_x, tap_mask
        )
        conv_bc = convolve(
            jnp.take(conv_bc_pool[0], rows_slot, axis=0),
            small_proj[:, :bc_width],
            kernel_bc,
            tap_mask,
        )
        conv_b = conv_bc[:, :half_width]
        conv_c = conv_bc[:, half_width:]
        step_size = jax.nn.softplus(step_raw + bias_heads[None, :])
        decay_rate = jnp.exp(-step_size * rate_heads[None, :])
        old_state = jnp.take(state_pool[0], rows_slot, axis=0) * alive[:, None, None, None]
        inner_heads = conv_x.reshape(micro_rows, heads_dev, head_size)
        new_state = (
            decay_rate[:, :, None, None] * old_state
            + (step_size[:, :, None] * inner_heads)[:, :, :, None] * conv_b[:, None, None, :]
        )
        read_out = (
            jnp.einsum("bhpn,bn->bhp", new_state, conv_c, precision=lax.Precision.HIGHEST)
            + skip_heads[None, :, None] * inner_heads
        )
        gated = read_out.reshape(micro_rows, chan_dev) * jax.nn.silu(gate_proj)
        square_sum = over_copies(jnp.sum(gated * gated, axis=1), "mp")
        normed = (
            gated
            * lax.rsqrt(square_sum[:, None] / (chan_dev * mp_count) + epsilon)
            * post_gain[None, :]
        ).astype(jnp.bfloat16)
        partial_value = jnp.dot(normed, proj_weights[2], preferred_element_type=jnp.float32)
        summed = over_copies_2(partial_value.astype(jnp.bfloat16), "mp").astype(jnp.float32)
        new_full = (residual + summed).astype(jnp.bfloat16)
        new_share = lax.dynamic_slice_in_dim(new_full, mp_index * model_share, model_share, 1)
        current_hidden = lax.dynamic_slice_in_dim(hidden_buffer, row_start, micro_rows, 0)
        hidden_buffer = lax.dynamic_update_slice_in_dim(
            hidden_buffer, jnp.where(in_range, new_share, current_hidden), row_start, 0
        )
        current_state = lax.dynamic_slice_in_dim(state_buffer, row_start, micro_rows, 0)
        state_buffer = lax.dynamic_update_slice_in_dim(
            state_buffer, jnp.where(in_range, new_state, current_state), row_start, 0
        )
        if tick_index + 1 < tick_count:
            received = passed_along(new_full, "section", 1)
    return (hidden_buffer[None], state_buffer[None])


def solution(mesh):
    placed = (
        P("dp", "mp"),
        P("dp"),
        P("dp"),
        P("section", None),
        P("section", None, "dp", "mp"),
        P("section", "dp", "mp"),
        P("section", None, "mp"),
        P("section", None, None),
        P("section", "dp", None, "mp"),
        P("section", "dp", None, None),
        P("section", "dp", "mp", None, None),
        P("section", "mp"),
        P("section", "mp"),
        P("section", "mp"),
        P("section", "mp"),
    )
    return jax.shard_map(
        local,
        mesh=mesh,
        in_specs=placed,
        out_specs=(P("section", "dp", "mp"), P("section", "dp", "mp", None, None)),
        check_vma=False,
    )
```

profile of v0, /device:TPU:128, one launch (start us, length us, event | category | flops | bytes accessed | tf_op | source)
XLA Modules:
  0.0 585.2 jit_solution(429785838524593616)
XLA Ops:
  9.4 5.8 all-to-all-start
  16.1 13.6 %all-gather = bf16[1,336,160]{2,0,1:T(2,128)(2,1)S(1)} all-gather(bf16[1,84,160]{2,0,1:T(2,128)(2,1)S(1)} %copy.74), channel_id=2, replica_groups=mesh['dp'=4,'mp'=16,'section'=4] {'dp'}, dimensions={1}, use_global_device_ids=true | all-gather | bytes 134400 | tf_op jit(solution)/shard_map/all_gather | solution.py:90
  31.4 8.1 %all-to-all-start.1 = ((bf16[16,1,1,336,160]{3,4,2,1,0:T(8,128)(2,1)}), bf16[16,1,1,336,160]{3,4,2,1,0:T(8,128)(2,1)}, u32[]{:S(2)}, u32[]{:S(2)}) async-start(bf16[16,1,1,336,160]{3,4,2,1,0:T(8,128)(2,1)} %broadcast_in_dim.79), calls=%async_computation.1 | async-start | bytes 3932160 | tf_op jit(solution)/shard_map/all_to_all | solution.py:12
  39.5 29.2 %all-gather.3.cloned.1.call-done = bf16[1,3,5120,160]{2,3,1,0:T(8,128)(2,1)} async-done(((bf16[1,3,1280,160]{2,3,1,0:T(8,128)(2,1)}), bf16[1,3,5120,160]{2,3,1,0:T(8,128)(2,1)}) %all-gather.3.cloned.1.call-update) | async-done | bytes 4915216 | tf_op jit(solution)/shard_map/all_gather | solution.py:89
  68.6 15.5 %copy.76 = bf16[1,3,5120,160]{3,1,0,2:T(4,128)(2,1)} copy(bf16[1,3,5120,160]{2,3,1,0:T(8,128)(2,1)} %all-gather.3.cloned.1.call-done) | data formatting | bytes 9830400 | tf_op jit(solution)/shard_map/all_gather | solution.py:89
  84.1 17.6 %reshape.822 = bf16[16,2,76800]{2,1,0:T(2,128)(2,1)} reshape(bf16[5120,1,3,160]{3,2,1,0:T(4,128)(2,1)} %bitcast.134) | data formatting | bytes 9830400
  101.8 5.7 all-to-all-start.2
  117.6 101.7 %all-to-all-done.2 = bf16[16,2,76800]{2,1,0:T(2,128)(2,1)} async-done(((bf16[16,2,76800]{2,1,0:T(2,128)(2,1)}), bf16[16,2,76800]{2,1,0:T(2,128)(2,1)}, u32[]{:S(2)}, u32[]{:S(2)}) %all-to-all-start.2) | async-done | bytes 4915232 | tf_op jit(solution)/shard_map/all_to_all | solution.py:92
  219.2 17.3 %reshape.823 = bf16[5120,1,3,160]{3,2,1,0:T(4,128)(2,1)} reshape(bf16[16,2,76800]{2,1,0:T(2,128)(2,1)} %all-to-all-done.2) | data formatting | bytes 9830400
  236.5 17.8 %copy.77 = bf16[1,3,16,320,160]{3,4,2,1,0:T(8,128)(2,1)} copy(bf16[1,3,16,320,160]{4,1,3,2,0:T(4,128)(2,1)} %bitcast.135) | data formatting | bytes 9830400 | tf_op jit(solution)/shard_map/all_to_all | solution.py:92
  254.3 5.2 fusion.188
  271.1 7.1 %all-to-all-done.3 = f32[16,1,4]{2,1,0:T(1,128)S(1)} async-done(((f32[16,1,4]{2,1,0:T(1,128)}), f32[16,1,4]{2,1,0:T(1,128)S(1)}, u32[]{:S(2)}, u32[]{:S(2)}) %all-to-all-start.3) | async-done | bytes 288 | tf_op jit(solution)/shard_map/all_to_all | solution.py:12
  309.9 3.8 collective-permute-done
  322.2 15.1 %all_to_all.102 = f32[16,1,4]{2,1,0:T(1,128)S(1)} all-to-all(f32[16,1,4]{2,1,0:T(1,128)S(1)} %broadcast_in_dim.82), channel_id=1, replica_groups=mesh['dp'=4,'mp'=16,'section'=4] {'mp'}, dimensions={0} | all-to-all | bytes 512 | tf_op jit(solution)/shard_map/all_to_all | solution.py:12
  339.6 12.8 %all_to_all.103 = bf16[16,4,2560]{2,1,0:T(4,128)(2,1)S(1)} all-to-all(bf16[16,4,2560]{2,1,0:T(4,128)(2,1)S(1)} %broadcast_in_dim.83), channel_id=1, replica_groups=mesh['dp'=4,'mp'=16,'section'=4] {'mp'}, dimensions={0} | all-to-all | bytes 655360 | tf_op jit(solution)/shard_map/all_to_all | solution.py:12
  356.2 5.4 collective-permute-done.1
  369.4 11.0 %all_to_all.104 = f32[16,1,4]{2,1,0:T(1,128)S(1)} all-to-all(f32[16,1,4]{2,1,0:T(1,128)S(1)} %broadcast_in_dim.84), channel_id=1, replica_groups=mesh['dp'=4,'mp'=16,'section'=4] {'mp'}, dimensions={0} | all-to-all | bytes 512 | tf_op jit(solution)/shard_map/all_to_all | solution.py:12
  382.7 12.6 %all_to_all.105 = bf16[16,4,2560]{2,1,0:T(4,128)(2,1)S(1)} all-to-all(bf16[16,4,2560]{2,1,0:T(4,128)(2,1)S(1)} %broadcast_in_dim.85), channel_id=1, replica_groups=mesh['dp'=4,'mp'=16,'section'=4] {'mp'}, dimensions={0} | all-to-all | bytes 655360 | tf_op jit(solution)/shard_map/all_to_all | solution.py:12
  399.1 5.4 collective-permute-done.2
  412.3 11.0 %all_to_all.106 = f32[16,1,4]{2,1,0:T(1,128)S(1)} all-to-all(f32[16,1,4]{2,1,0:T(1,128)S(1)} %broadcast_in_dim.86), channel_id=1, replica_groups=mesh['dp'=4,'mp'=16,'section'=4] {'mp'}, dimensions={0} | all-to-all | bytes 512 | tf_op jit(solution)/shard_map/all_to_all | solution.py:12
  434.8 5.1 all-to-all-done.10
  445.1 4.1 collective-permute-done.3
  460.9 7.0 %all-to-all-done.11 = f32[16,1,4]{2,1,0:T(1,128)S(1)} async-done(((f32[16,1,4]{2,1,0:T(1,128)}), f32[16,1,4]{2,1,0:T(1,128)S(1)}, u32[]{:S(2)}, u32[]{:S(2)}) %all-to-all-start.11) | async-done | bytes 288 | tf_op jit(solution)/shard_map/all_to_all | solution.py:12
  470.9 3.7 all-to-all-start.12
  479.6 5.0 all-to-all-done.12
  489.4 4.4 collective-permute-done.4
  504.9 7.6 %all-to-all-done.13 = f32[16,1,4]{2,1,0:T(1,128)S(1)} async-done(((f32[16,1,4]{2,1,0:T(1,128)}), f32[16,1,4]{2,1,0:T(1,128)S(1)}, u32[]{:S(2)}, u32[]{:S(2)}) %all-to-all-start.13) | async-done | bytes 288 | tf_op jit(solution)/shard_map/all_to_all | solution.py:12
  524.0 3.6 copy.142
  531.3 7.0 %collective-permute-done.5 = bf16[4,2560]{1,0:T(4,128)(2,1)S(1)} collective-permute-done((bf16[4,2560]{1,0:T(4,128)(2,1)S(1)}, bf16[4,2560]{1,0:T(4,128)(2,1)S(1)}, u32[]{:S(2)}, u32[]{:S(2)}) %collective-permute-start.5) | collective-permute-done | bytes 20512 | tf_op jit(solution)/shard_map/ppermute | solution.py:39
  547.3 5.9 %all-to-all-start.15 = ((f32[16,1,4]{2,1,0:T(1,128)}), f32[16,1,4]{2,1,0:T(1,128)S(1)}, u32[]{:S(2)}, u32[]{:S(2)}) async-start(f32[16,1,4]{2,1,0:T(1,128)} %broadcast_in_dim.93), calls=%async_computation.15 | async-start | bytes 16384 | tf_op jit(solution)/shard_map/all_to_all | solution.py:12
  555.6 5.4 all-to-all-done.15
  567.6 9.9 %all-to-all-done.16 = bf16[16,4,2560]{2,1,0:T(4,128)(2,1)S(1)} async-done(((bf16[16,4,2560]{2,1,0:T(4,128)(2,1)}), bf16[16,4,2560]{2,1,0:T(4,128)(2,1)S(1)}, u32[]{:S(2)}, u32[]{:S(2)}) %all-to-all-start.16) | async-done | bytes 327712 | tf_op jit(solution)/shard_map/all_to_all | solution.py:12
  (383 shorter events, 179.5 us)
Async XLA Ops:
  7.2 104.1 %copy-start = (f32[1,18,5,64,128]{4,3,2,1,0:T(8,128)S(1)}, f32[1,18,5,64,128]{4,3,2,1,0:T(8,128)}, u32[]{:S(2)}) copy-start(f32[1,18,5,64,128]{4,3,2,1,0:T(8,128)} %param.31) | copy-start | bytes 8847364
  7.2 61.5 %all-gather.3.cloned.1.call-start = ((), (), s32[]{:S(2)}) async-start(), calls=%async_computation.17 | async-start | bytes 6144000 | tf_op jit(solution)/shard_map/all_gather | solution.py:89
  9.4 20.5 %all-to-all-start = ((bf16[16,16,160]{2,1,0:T(8,128)(2,1)}), bf16[16,16,160]{2,1,0:T(8,128)(2,1)S(1)}, u32[]{:S(2)}, u32[]{:S(2)}) async-start(bf16[16,16,160]{2,1,0:T(8,128)(2,1)} %broadcast_in_dim.76), calls=%async_computation | async-start | bytes 262144 | tf_op jit(solution)/shard_map/all_to_all | solution.py:12
  31.4 70.4 %all-to-all-start.1 = ((bf16[16,1,1,336,160]{3,4,2,1,0:T(8,128)(2,1)}), bf16[16,1,1,336,160]{3,4,2,1,0:T(8,128)(2,1)}, u32[]{:S(2)}, u32[]{:S(2)}) async-start(bf16[16,1,1,336,160]{3,4,2,1,0:T(8,128)(2,1)} %broadcast_in_dim.79), calls=%async_computation.1 | async-start | bytes 3932160 | tf_op jit(solution)/shard_map/all_to_all | solution.py:12
  101.8 117.4 %all-to-all-start.2 = ((bf16[16,2,76800]{2,1,0:T(2,128)(2,1)}), bf16[16,2,76800]{2,1,0:T(2,128)(2,1)}, u32[]{:S(2)}, u32[]{:S(2)}) async-start(bf16[16,2,76800]{2,1,0:T(2,128)(2,1)} %reshape.822), calls=%async_computation.2 | async-start | bytes 9830400 | tf_op jit(solution)/shard_map/all_to_all | solution.py:92
  108.4 153.0 %copy-start.59 = (pred[4]{0:T(512)(128)(4,1)}, pred[4]{0:T(512)(128)(4,1)S(1)}, u32[]{:S(2)}) copy-start(pred[4]{0:T(512)(128)(4,1)S(1)} %get-tuple-element.98) | copy-start | bytes 16
  108.4 153.0 %copy-start.71 = (f32[4]{0:T(128)}, f32[4]{0:T(128)S(1)}, u32[]{:S(2)}) copy-start(f32[4]{0:T(128)S(1)} %get-tuple-element.133) | copy-start | bytes 52
  111.2 125.2 %copy-start.18 = (f32[1,1,256]{2,1,0:T(1,128)}, f32[1,1,256]{2,1,0:T(1,128)S(1)}, u32[]{:S(2)}) copy-start(f32[1,1,256]{2,1,0:T(1,128)S(1)} %slice.161) | copy-start | bytes 3076
  113.9 145.7 %copy-start.15 = (f32[320]{0:T(512)}, f32[320]{0:T(512)S(1)}, u32[]{:S(2)}) copy-start(f32[320]{0:T(512)S(1)} %slice_reduce_fusion) | copy-start | bytes 3844
  114.6 187.6 %copy-start.39 = (f32[4,3]{1,0:T(4,128)}, f32[4,3]{1,0:T(4,128)S(1)}, u32[]{:S(2)}) copy-start(f32[4,3]{1,0:T(4,128)S(1)} %get-tuple-element.100) | copy-start | bytes 148
  117.5 143.9 %copy-start.51 = (f32[4,5]{1,0:T(4,128)}, f32[4,5]{1,0:T(4,128)S(1)}, u32[]{:S(2)}) copy-start(f32[4,5]{1,0:T(4,128)S(1)} %get-tuple-element.61) | copy-start | bytes 244
  117.5 143.8 %copy-start.53 = (f32[4,128]{1,0:T(4,128)}, f32[4,128]{1,0:T(4,128)S(1)}, u32[]{:S(2)}) copy-start(f32[4,128]{1,0:T(4,128)S(1)} %get-tuple-element.86) | copy-start | bytes 6148
  266.4 19.0 %copy-start.13 = (bf16[1,18,3,320]{3,2,1,0:T(4,128)(2,1)S(1)}, bf16[1,18,3,320]{3,2,1,0:T(4,128)(2,1)}, u32[]{:S(2)}) copy-start(bf16[1,18,3,320]{3,2,1,0:T(4,128)(2,1)} %param.29) | copy-start | bytes 103684
  266.4 19.7 %copy-start.17 = (bf16[1,18,3,256]{3,2,1,0:T(4,128)(2,1)S(1)}, bf16[1,18,3,256]{3,2,1,0:T(4,128)(2,1)}, u32[]{:S(2)}) copy-start(bf16[1,18,3,256]{3,2,1,0:T(4,128)(2,1)} %param.30) | copy-start | bytes 82948
  266.4 35.8 %copy-start.23 = (f32[3,320]{1,0:T(4,128)S(1)}, f32[3,320]{1,0:T(4,128)}, u32[]{:S(2)}) copy-start(f32[3,320]{1,0:T(4,128)} %copy-done.22) | copy-start | bytes 11524
  267.0 11.2 %all-to-all-start.3 = ((f32[16,1,4]{2,1,0:T(1,128)}), f32[16,1,4]{2,1,0:T(1,128)S(1)}, u32[]{:S(2)}, u32[]{:S(2)}) async-start(f32[16,1,4]{2,1,0:T(1,128)} %broadcast_in_dim.80), calls=%async_computation.3 | async-start | bytes 16384 | tf_op jit(solution)/shard_map/all_to_all | solution.py:12
  281.2 23.3 %all-to-all-start.4 = ((bf16[16,4,2560]{2,1,0:T(4,128)(2,1)}), bf16[16,4,2560]{2,1,0:T(4,128)(2,1)S(1)}, u32[]{:S(2)}, u32[]{:S(2)}) async-start(bf16[16,4,2560]{2,1,0:T(4,128)(2,1)} %broadcast_in_dim.81), calls=%async_computation.4 | async-start | bytes 655360 | tf_op jit(solution)/shard_map/all_to_all | solution.py:12
  304.7 9.0 %collective-permute-start = (bf16[4,2560]{1,0:T(4,128)(2,1)S(1)}, bf16[4,2560]{1,0:T(4,128)(2,1)S(1)}, u32[]{:S(2)}, u32[]{:S(2)}) collective-permute-start(bf16[4,2560]{1,0:T(4,128)(2,1)S(1)} %add_convert_fusion), channel_id=1, source_target_pairs={{0,1},{1,2},{2,3},{4,5},{5,6},{6,7},{8,9},{9,10},{10,11},{12,13},{... | collective-permute-start | bytes 61448 | tf_op jit(solution)/shard_map/ppermute | solution.py:39
  352.5 9.0 %collective-permute-start.1 = (bf16[4,2560]{1,0:T(4,128)(2,1)S(1)}, bf16[4,2560]{1,0:T(4,128)(2,1)S(1)}, u32[]{:S(2)}, u32[]{:S(2)}) collective-permute-start(bf16[4,2560]{1,0:T(4,128)(2,1)S(1)} %fusion.80), channel_id=1, source_target_pairs={{0,1},{1,2},{2,3},{4,5},{5,6},{6,7},{8,9},{9,10},{10,11},{12,13},{... | collective-permute-start | bytes 61448 | tf_op jit(solution)/shard_map/ppermute | solution.py:39
  395.5 9.0 %collective-permute-start.2 = (bf16[4,2560]{1,0:T(4,128)(2,1)S(1)}, bf16[4,2560]{1,0:T(4,128)(2,1)S(1)}, u32[]{:S(2)}, u32[]{:S(2)}) collective-permute-start(bf16[4,2560]{1,0:T(4,128)(2,1)S(1)} %fusion.84), channel_id=1, source_target_pairs={{0,1},{1,2},{2,3},{4,5},{5,6},{6,7},{8,9},{9,10},{10,11},{12,13},{... | collective-permute-start | bytes 61448 | tf_op jit(solution)/shard_map/ppermute | solution.py:39
  426.4 13.5 %all-to-all-start.10 = ((bf16[16,4,2560]{2,1,0:T(4,128)(2,1)}), bf16[16,4,2560]{2,1,0:T(4,128)(2,1)S(1)}, u32[]{:S(2)}, u32[]{:S(2)}) async-start(bf16[16,4,2560]{2,1,0:T(4,128)(2,1)} %broadcast_in_dim.87), calls=%async_computation.10 | async-start | bytes 655360 | tf_op jit(solution)/shard_map/all_to_all | solution.py:12
  440.1 9.1 %collective-permute-start.3 = (bf16[4,2560]{1,0:T(4,128)(2,1)S(1)}, bf16[4,2560]{1,0:T(4,128)(2,1)S(1)}, u32[]{:S(2)}, u32[]{:S(2)}) collective-permute-start(bf16[4,2560]{1,0:T(4,128)(2,1)S(1)} %fusion.88), channel_id=1, source_target_pairs={{0,1},{1,2},{2,3},{4,5},{5,6},{6,7},{8,9},{9,10},{10,11},{12,13},{... | collective-permute-start | bytes 61448 | tf_op jit(solution)/shard_map/ppermute | solution.py:39
  456.1 18.6 %copy-start.50 = (pred[4]{0:T(512)(128)(4,1)S(1)}, pred[4]{0:T(512)(128)(4,1)}, u32[]{:S(2)}) copy-start(pred[4]{0:T(512)(128)(4,1)} %get-tuple-element.96) | copy-start | bytes 16
  456.1 18.6 %copy-start.56 = (f32[4,5]{1,0:T(4,128)S(1)}, f32[4,5]{1,0:T(4,128)}, u32[]{:S(2)}) copy-start(f32[4,5]{1,0:T(4,128)} %copy-done.55) | copy-start | bytes 244
  456.7 11.2 %all-to-all-start.11 = ((f32[16,1,4]{2,1,0:T(1,128)}), f32[16,1,4]{2,1,0:T(1,128)S(1)}, u32[]{:S(2)}, u32[]{:S(2)}) async-start(f32[16,1,4]{2,1,0:T(1,128)} %broadcast_in_dim.88), calls=%async_computation.11 | async-start | bytes 16384 | tf_op jit(solution)/shard_map/all_to_all | solution.py:12
  470.9 13.6 %all-to-all-start.12 = ((bf16[16,4,2560]{2,1,0:T(4,128)(2,1)}), bf16[16,4,2560]{2,1,0:T(4,128)(2,1)S(1)}, u32[]{:S(2)}, u32[]{:S(2)}) async-start(bf16[16,4,2560]{2,1,0:T(4,128)(2,1)} %broadcast_in_dim.89), calls=%async_computation.12 | async-start | bytes 655360 | tf_op jit(solution)/shard_map/all_to_all | solution.py:12
  484.7 9.1 %collective-permute-start.4 = (bf16[4,2560]{1,0:T(4,128)(2,1)S(1)}, bf16[4,2560]{1,0:T(4,128)(2,1)S(1)}, u32[]{:S(2)}, u32[]{:S(2)}) collective-permute-start(bf16[4,2560]{1,0:T(4,128)(2,1)S(1)} %fusion.92), channel_id=1, source_target_pairs={{0,1},{1,2},{2,3},{4,5},{5,6},{6,7},{8,9},{9,10},{10,11},{12,13},{... | collective-permute-start | bytes 61448 | tf_op jit(solution)/shard_map/ppermute | solution.py:39
  501.3 11.2 %all-to-all-start.13 = ((f32[16,1,4]{2,1,0:T(1,128)}), f32[16,1,4]{2,1,0:T(1,128)S(1)}, u32[]{:S(2)}, u32[]{:S(2)}) async-start(f32[16,1,4]{2,1,0:T(1,128)} %broadcast_in_dim.90), calls=%async_computation.13 | async-start | bytes 16384 | tf_op jit(solution)/shard_map/all_to_all | solution.py:12
  515.6 13.5 %all-to-all-start.14 = ((bf16[16,4,2560]{2,1,0:T(4,128)(2,1)}), bf16[16,4,2560]{2,1,0:T(4,128)(2,1)S(1)}, u32[]{:S(2)}, u32[]{:S(2)}) async-start(bf16[16,4,2560]{2,1,0:T(4,128)(2,1)} %broadcast_in_dim.91), calls=%async_computation.14 | async-start | bytes 655360 | tf_op jit(solution)/shard_map/all_to_all | solution.py:12
  529.3 9.0 %collective-permute-start.5 = (bf16[4,2560]{1,0:T(4,128)(2,1)S(1)}, bf16[4,2560]{1,0:T(4,128)(2,1)S(1)}, u32[]{:S(2)}, u32[]{:S(2)}) collective-permute-start(bf16[4,2560]{1,0:T(4,128)(2,1)S(1)} %fusion.96), channel_id=1, source_target_pairs={{0,1},{1,2},{2,3},{4,5},{5,6},{6,7},{8,9},{9,10},{10,11},{12,13},{... | collective-permute-start | bytes 61448 | tf_op jit(solution)/shard_map/ppermute | solution.py:39
  547.3 13.7 %all-to-all-start.15 = ((f32[16,1,4]{2,1,0:T(1,128)}), f32[16,1,4]{2,1,0:T(1,128)S(1)}, u32[]{:S(2)}, u32[]{:S(2)}) async-start(f32[16,1,4]{2,1,0:T(1,128)} %broadcast_in_dim.93), calls=%async_computation.15 | async-start | bytes 16384 | tf_op jit(solution)/shard_map/all_to_all | solution.py:12
  564.0 13.5 %all-to-all-start.16 = ((bf16[16,4,2560]{2,1,0:T(4,128)(2,1)}), bf16[16,4,2560]{2,1,0:T(4,128)(2,1)S(1)}, u32[]{:S(2)}, u32[]{:S(2)}) async-start(bf16[16,4,2560]{2,1,0:T(4,128)(2,1)} %broadcast_in_dim.94), calls=%async_computation.16 | async-start | bytes 655360 | tf_op jit(solution)/shard_map/all_to_all | solution.py:12
  (63 other events, 403.0 us)
Sparse Core Ops, SparseCore 0:
  9.8 58.7 all-gather.2
where the time goes:
time: 590 us; the launch traced here: 585 us
  waiting for transfers between devices  210 us (36%)
  local copies, waits for them, and re-layouts  122 us (21%)
  blocking collectives  76.2 us (13%)
  starting transfers between devices  65.7 us (11%)
  matrix products  63.9 us (11%)
  other arithmetic  31.3 us (5%)
  between operations  15.4 us (3%)
    all_to_all x1, waiting for transfers between devices, local(): lax.all_to_all(zxo_rows, 'mp', split_axis=2, concat_axis=3, tiled=True)[0]  102 us
    all_to_all x5, blocking collectives, copy_for_each(): lax.all_to_all(jnp.broadcast_to(array[None], (devices, *array.shape)), ax...  62.5 us
    all_to_all x11, waiting for transfers between devices, copy_for_each(): lax.all_to_all(jnp.broadcast_to(array[None], (devices, *array.shape)), ax...  48.7 us
    all_to_all x11, starting transfers between devices, copy_for_each(): lax.all_to_all(jnp.broadcast_to(array[None], (devices, *array.shape)), ax...  48 us
    unnamed x157, local copies, waits for them, and re-layouts  42.3 us
    dot_general x21, matrix products, project(): lax.dot_general(inputs, weights, (((1,), (1,)), ((), ())), preferred_elem...  33 us
    ppermute x6, waiting for transfers between devices, passed_along(): return lax.ppermute(array, axis, pairs)  30.1 us
    all_gather x1, waiting for transfers between devices, local(): lax.all_gather(w_zxo, 'dp', axis=2, tiled=True)  29.2 us
  transfers between devices with their start and end apart: 19, of which 16 were waited for; matrix products, arithmetic and copies ran while one was open for 17% of the time, Pallas kernels for 0%

commit v1 on v0

--- a/solution.py
+++ b/solution.py
@@ -86,7 +86,12 @@
     bc_width = conv_bc_weight.shape[2]
     half_width = bc_width // 2
     zxo_rows, small_rows = (
-        lax.all_gather(w_zxo, "dp", axis=2, tiled=True),
+        jnp.concatenate(
+            lax.all_to_all(
+                jnp.stack([w_zxo] * lax.psum(1, "dp")), "dp", split_axis=0, concat_axis=0
+            ),
+            axis=2,
+        ),
         lax.all_gather(w_bcdt[:, None], "dp", axis=2, tiled=True),
     )
     proj_weights = lax.all_to_all(zxo_rows, "mp", split_axis=2, concat_axis=3, tiled=True)[0]

time: 590 us -> 618 us (1.047)
  blocking collectives: 76.2 us -> 139 us
  waiting for transfers between devices: 210 us -> 191 us
  between operations: 15.4 us -> 1.99 us
    all_gather x1, blocking collectives: 13.6 us -> 62.3 us  [local(): lax.all_gather(w_bcdt[:, None], 'dp', axis=2, tiled=True)]
    all_gather x1 -> x0, waiting for transfers between devices: 29.2 us -> none  [local(): lax.all_gather(w_zxo, 'dp', axis=2, tiled=True)]
    reshape x0 -> x1, local copies, waits for them, and re-layouts: none -> 15.5 us  [local(): jnp.concatenate(lax.all_to_all(jnp.stack([w_zxo] * lax.psum(1, 'dp')), 'd...]
    all_gather x1 -> x0, local copies, waits for them, and re-layouts: 15.5 us -> none  [local(): lax.all_gather(w_zxo, 'dp', axis=2, tiled=True)]
    all_to_all x5 -> x6, blocking collectives: 62.5 us -> 76.5 us  [copy_for_each(): lax.all_to_all(jnp.broadcast_to(array[None], (devices, *array.shape)), ax...]
    all_to_all x11 -> x10, waiting for transfers between devices: 48.7 us -> 58.7 us  [copy_for_each(): lax.all_to_all(jnp.broadcast_to(array[None], (devices, *array.shape)), ax...]
    all_to_all x11 -> x10, starting transfers between devices: 48 us -> 38.6 us  [copy_for_each(): lax.all_to_all(jnp.broadcast_to(array[None], (devices, *array.shape)), ax...]
    unnamed x157 -> x159, local copies, waits for them, and re-layouts: 42.3 us -> 41.6 us
  transfers between devices with their start and end apart: 19 -> 18, of which waited for: 16 -> 16; matrix products, arithmetic and copies ran while one was open for 17% -> 16% of each run, Pallas kernels for 0% -> 0%
where the time goes in v1:
time: 618 us; the launch traced here: 613 us
  waiting for transfers between devices  191 us (31%)
  blocking collectives  139 us (22%)
  local copies, waits for them, and re-layouts  125 us (20%)
  matrix products  63.9 us (10%)
  starting transfers between devices  60.3 us (10%)
  other arithmetic  31.3 us (5%)
    all_to_all x1, waiting for transfers between devices, local(): lax.all_to_all(zxo_rows, 'mp', split_axis=2, concat_axis=3, tiled=True)[0]  103 us
    all_to_all x6, blocking collectives, copy_for_each(): lax.all_to_all(jnp.broadcast_to(array[None], (devices, *array.shape)), ax...  76.5 us
    all_gather x1, blocking collectives, local(): lax.all_gather(w_bcdt[:, None], 'dp', axis=2, tiled=True)  62.3 us
    all_to_all x10, waiting for transfers between devices, copy_for_each(): lax.all_to_all(jnp.broadcast_to(array[None], (devices, *array.shape)), ax...  58.7 us
    unnamed x159, local copies, waits for them, and re-layouts  41.6 us
    all_to_all x10, starting transfers between devices, copy_for_each(): lax.all_to_all(jnp.broadcast_to(array[None], (devices, *array.shape)), ax...  38.6 us
    dot_general x21, matrix products, project(): lax.dot_general(inputs, weights, (((1,), (1,)), ((), ())), preferred_elem...  33 us
    ppermute x6, waiting for transfers between devices, passed_along(): return lax.ppermute(array, axis, pairs)  30 us
  transfers between devices with their start and end apart: 18, of which 16 were waited for; matrix products, arithmetic and copies ran while one was open for 16% of the time, Pallas kernels for 0%

profile of v1, /device:TPU:128, one launch (start us, length us, event | category | flops | bytes accessed | tf_op | source)
XLA Modules:
  0.0 612.6 jit_solution(11823452913391581471)
XLA Ops:
  1.5 14.1 %all_to_all.107 = bf16[16,16,160]{2,1,0:T(8,128)(2,1)S(1)} all-to-all(bf16[16,16,160]{2,1,0:T(8,128)(2,1)S(1)} %broadcast_in_dim.76), channel_id=1, replica_groups=mesh['dp'=4,'mp'=16,'section'=4] {'mp'}, dimensions={0} | all-to-all | bytes 163840 | tf_op jit(solution)/shard_map/all_to_all | solution.py:12
  15.6 3.9 stack.2
  19.5 5.1 all-to-all-start.2
  24.8 62.3 %all-gather = bf16[1,336,160]{2,0,1:T(2,128)(2,1)S(1)} all-gather(bf16[1,84,160]{2,0,1:T(2,128)(2,1)S(1)} %copy.70), channel_id=2, replica_groups=mesh['dp'=4,'mp'=16,'section'=4] {'dp'}, dimensions={1}, use_global_device_ids=true | all-gather | bytes 134400 | tf_op jit(solution)/shard_map/all_gather | solution.py:95
  88.8 4.4 all-to-all-start.1
  93.2 15.5 %copy.103 = bf16[1,3,4,1280,160]{4,1,3,2,0:T(4,128)(2,1)} copy(bf16[1,3,4,1280,160]{3,4,1,0,2:T(8,128)(2,1)} %bitcast.10) | data formatting | bytes 9830400 | tf_op jit(solution)/shard_map/reshape | solution.py:89
  108.7 17.6 %reshape.833 = bf16[16,2,76800]{2,1,0:T(2,128)(2,1)} reshape(bf16[5120,1,3,160]{3,2,1,0:T(4,128)(2,1)} %bitcast.137) | data formatting | bytes 9830400
  126.4 10.1 %all-to-all-done.1 = bf16[16,1,1,336,160]{3,4,2,1,0:T(8,128)(2,1)} async-done(((bf16[16,1,1,336,160]{3,4,2,1,0:T(8,128)(2,1)}), bf16[16,1,1,336,160]{3,4,2,1,0:T(8,128)(2,1)}, u32[]{:S(2)}, u32[]{:S(2)}) %all-to-all-start.1) | async-done | bytes 1720352 | tf_op jit(solution)/shard_map/all_to_all | solution.py:12
  136.5 4.6 all-to-all-start.3
  151.2 102.5 %all-to-all-done.3 = bf16[16,2,76800]{2,1,0:T(2,128)(2,1)} async-done(((bf16[16,2,76800]{2,1,0:T(2,128)(2,1)}), bf16[16,2,76800]{2,1,0:T(2,128)(2,1)}, u32[]{:S(2)}, u32[]{:S(2)}) %all-to-all-start.3) | async-done | bytes 4915232 | tf_op jit(solution)/shard_map/all_to_all | solution.py:97
  253.7 17.3 %reshape.834 = bf16[5120,1,3,160]{3,2,1,0:T(4,128)(2,1)} reshape(bf16[16,2,76800]{2,1,0:T(2,128)(2,1)} %all-to-all-done.3) | data formatting | bytes 9830400
  271.0 17.8 %copy.74 = bf16[1,3,16,320,160]{3,4,2,1,0:T(8,128)(2,1)} copy(bf16[1,3,16,320,160]{4,1,3,2,0:T(4,128)(2,1)} %bitcast.138) | data formatting | bytes 9830400 | tf_op jit(solution)/shard_map/all_to_all | solution.py:97
  288.8 5.2 fusion.188
  305.6 7.1 %all-to-all-done.4 = f32[16,1,4]{2,1,0:T(1,128)S(1)} async-done(((f32[16,1,4]{2,1,0:T(1,128)}), f32[16,1,4]{2,1,0:T(1,128)S(1)}, u32[]{:S(2)}, u32[]{:S(2)}) %all-to-all-start.4) | async-done | bytes 288 | tf_op jit(solution)/shard_map/all_to_all | solution.py:12
  344.4 3.8 collective-permute-done
  356.6 15.1 %all_to_all.108 = f32[16,1,4]{2,1,0:T(1,128)S(1)} all-to-all(f32[16,1,4]{2,1,0:T(1,128)S(1)} %broadcast_in_dim.82), channel_id=1, replica_groups=mesh['dp'=4,'mp'=16,'section'=4] {'mp'}, dimensions={0} | all-to-all | bytes 512 | tf_op jit(solution)/shard_map/all_to_all | solution.py:12
  374.1 12.6 %all_to_all.109 = bf16[16,4,2560]{2,1,0:T(4,128)(2,1)S(1)} all-to-all(bf16[16,4,2560]{2,1,0:T(4,128)(2,1)S(1)} %broadcast_in_dim.83), channel_id=1, replica_groups=mesh['dp'=4,'mp'=16,'section'=4] {'mp'}, dimensions={0} | all-to-all | bytes 655360 | tf_op jit(solution)/shard_map/all_to_all | solution.py:12
  390.5 5.3 collective-permute-done.1
  403.7 11.0 %all_to_all.110 = f32[16,1,4]{2,1,0:T(1,128)S(1)} all-to-all(f32[16,1,4]{2,1,0:T(1,128)S(1)} %broadcast_in_dim.84), channel_id=1, replica_groups=mesh['dp'=4,'mp'=16,'section'=4] {'mp'}, dimensions={0} | all-to-all | bytes 512 | tf_op jit(solution)/shard_map/all_to_all | solution.py:12
  417.0 12.6 %all_to_all.111 = bf16[16,4,2560]{2,1,0:T(4,128)(2,1)S(1)} all-to-all(bf16[16,4,2560]{2,1,0:T(4,128)(2,1)S(1)} %broadcast_in_dim.85), channel_id=1, replica_groups=mesh['dp'=4,'mp'=16,'section'=4] {'mp'}, dimensions={0} | all-to-all | bytes 655360 | tf_op jit(solution)/shard_map/all_to_all | solution.py:12
  433.3 5.4 collective-permute-done.2
  446.6 11.0 %all_to_all.112 = f32[16,1,4]{2,1,0:T(1,128)S(1)} all-to-all(f32[16,1,4]{2,1,0:T(1,128)S(1)} %broadcast_in_dim.86), channel_id=1, replica_groups=mesh['dp'=4,'mp'=16,'section'=4] {'mp'}, dimensions={0} | all-to-all | bytes 512 | tf_op jit(solution)/shard_map/all_to_all | solution.py:12
  469.1 5.0 all-to-all-done.11
  479.4 4.1 collective-permute-done.3
  495.2 7.0 %all-to-all-done.12 = f32[16,1,4]{2,1,0:T(1,128)S(1)} async-done(((f32[16,1,4]{2,1,0:T(1,128)}), f32[16,1,4]{2,1,0:T(1,128)S(1)}, u32[]{:S(2)}, u32[]{:S(2)}) %all-to-all-start.12) | async-done | bytes 288 | tf_op jit(solution)/shard_map/all_to_all | solution.py:12
  513.8 5.0 all-to-all-done.13
  523.7 4.4 collective-permute-done.4
  539.2 7.6 %all-to-all-done.14 = f32[16,1,4]{2,1,0:T(1,128)S(1)} async-done(((f32[16,1,4]{2,1,0:T(1,128)}), f32[16,1,4]{2,1,0:T(1,128)S(1)}, u32[]{:S(2)}, u32[]{:S(2)}) %all-to-all-start.14) | async-done | bytes 288 | tf_op jit(solution)/shard_map/all_to_all | solution.py:12
  565.6 7.0 %collective-permute-done.5 = bf16[4,2560]{1,0:T(4,128)(2,1)S(1)} collective-permute-done((bf16[4,2560]{1,0:T(4,128)(2,1)S(1)}, bf16[4,2560]{1,0:T(4,128)(2,1)S(1)}, u32[]{:S(2)}, u32[]{:S(2)}) %collective-permute-start.5) | collective-permute-done | bytes 20512 | tf_op jit(solution)/shard_map/ppermute | solution.py:39
  581.5 5.9 all-to-all-start.16
  589.9 5.4 all-to-all-done.16
  601.9 9.9 %all-to-all-done.17 = bf16[16,4,2560]{2,1,0:T(4,128)(2,1)S(1)} async-done(((bf16[16,4,2560]{2,1,0:T(4,128)(2,1)}), bf16[16,4,2560]{2,1,0:T(4,128)(2,1)S(1)}, u32[]{:S(2)}, u32[]{:S(2)}) %all-to-all-start.17) | async-done | bytes 327712 | tf_op jit(solution)/shard_map/all_to_all | solution.py:12
  (384 shorter events, 184.7 us)
Async XLA Ops:
  0.6 144.2 %copy-start = (f32[1,18,5,64,128]{4,3,2,1,0:T(8,128)S(1)}, f32[1,18,5,64,128]{4,3,2,1,0:T(8,128)}, u32[]{:S(2)}) copy-start(f32[1,18,5,64,128]{4,3,2,1,0:T(8,128)} %param.31) | copy-start | bytes 8847364
  19.5 67.8 %all-to-all-start.2 = ((bf16[4,1,3,1280,160]{3,4,2,1,0:T(8,128)(2,1)}), bf16[4,1,3,1280,160]{3,4,2,1,0:T(8,128)(2,1)}, u32[]{:S(2)}, u32[]{:S(2)}) async-start(bf16[4,1,3,1280,160]{3,4,2,1,0:T(8,128)(2,1)} %stack.2), calls=%async_computation.2 | async-start | bytes 9830400 | tf_op jit(solution)/shard_map/all_to_all | solution.py:90
  88.8 47.7 %all-to-all-start.1 = ((bf16[16,1,1,336,160]{3,4,2,1,0:T(8,128)(2,1)}), bf16[16,1,1,336,160]{3,4,2,1,0:T(8,128)(2,1)}, u32[]{:S(2)}, u32[]{:S(2)}) async-start(bf16[16,1,1,336,160]{3,4,2,1,0:T(8,128)(2,1)} %broadcast_in_dim.79), calls=%async_computation.1 | async-start | bytes 3932160 | tf_op jit(solution)/shard_map/all_to_all | solution.py:12
  126.4 21.1 %copy-start.44 = (f32[1,4,320]{2,1,0:T(4,128)S(1)}, f32[1,4,320]{2,1,0:T(4,128)}, u32[]{:S(2)}) copy-start(f32[1,4,320]{2,1,0:T(4,128)} %param.27) | copy-start | bytes 15364
  136.5 117.2 %all-to-all-start.3 = ((bf16[16,2,76800]{2,1,0:T(2,128)(2,1)}), bf16[16,2,76800]{2,1,0:T(2,128)(2,1)}, u32[]{:S(2)}, u32[]{:S(2)}) async-start(bf16[16,2,76800]{2,1,0:T(2,128)(2,1)} %reshape.833), calls=%async_computation.3 | async-start | bytes 9830400 | tf_op jit(solution)/shard_map/all_to_all | solution.py:97
  142.0 153.8 %copy-start.60 = (pred[4]{0:T(512)(128)(4,1)}, pred[4]{0:T(512)(128)(4,1)S(1)}, u32[]{:S(2)}) copy-start(pred[4]{0:T(512)(128)(4,1)S(1)} %get-tuple-element.98) | copy-start | bytes 16
  142.1 153.8 %copy-start.72 = (f32[4]{0:T(128)}, f32[4]{0:T(128)S(1)}, u32[]{:S(2)}) copy-start(f32[4]{0:T(128)S(1)} %get-tuple-element.133) | copy-start | bytes 52
  144.9 126.1 %copy-start.18 = (f32[1,1,256]{2,1,0:T(1,128)}, f32[1,1,256]{2,1,0:T(1,128)S(1)}, u32[]{:S(2)}) copy-start(f32[1,1,256]{2,1,0:T(1,128)S(1)} %slice.161) | copy-start | bytes 3076
  147.5 146.5 %copy-start.15 = (f32[320]{0:T(512)}, f32[320]{0:T(512)S(1)}, u32[]{:S(2)}) copy-start(f32[320]{0:T(512)S(1)} %slice_reduce_fusion) | copy-start | bytes 3844
  148.2 188.4 %copy-start.40 = (f32[4,3]{1,0:T(4,128)}, f32[4,3]{1,0:T(4,128)S(1)}, u32[]{:S(2)}) copy-start(f32[4,3]{1,0:T(4,128)S(1)} %get-tuple-element.100) | copy-start | bytes 148
  151.2 144.7 %copy-start.52 = (f32[4,5]{1,0:T(4,128)}, f32[4,5]{1,0:T(4,128)S(1)}, u32[]{:S(2)}) copy-start(f32[4,5]{1,0:T(4,128)S(1)} %get-tuple-element.61) | copy-start | bytes 244
  151.2 144.7 %copy-start.54 = (f32[4,128]{1,0:T(4,128)}, f32[4,128]{1,0:T(4,128)S(1)}, u32[]{:S(2)}) copy-start(f32[4,128]{1,0:T(4,128)S(1)} %get-tuple-element.86) | copy-start | bytes 6148
  300.9 19.0 %copy-start.13 = (bf16[1,18,3,320]{3,2,1,0:T(4,128)(2,1)S(1)}, bf16[1,18,3,320]{3,2,1,0:T(4,128)(2,1)}, u32[]{:S(2)}) copy-start(bf16[1,18,3,320]{3,2,1,0:T(4,128)(2,1)} %param.29) | copy-start | bytes 103684
  300.9 19.7 %copy-start.17 = (bf16[1,18,3,256]{3,2,1,0:T(4,128)(2,1)S(1)}, bf16[1,18,3,256]{3,2,1,0:T(4,128)(2,1)}, u32[]{:S(2)}) copy-start(bf16[1,18,3,256]{3,2,1,0:T(4,128)(2,1)} %param.30) | copy-start | bytes 82948
  300.9 35.7 %copy-start.23 = (f32[3,320]{1,0:T(4,128)S(1)}, f32[3,320]{1,0:T(4,128)}, u32[]{:S(2)}) copy-start(f32[3,320]{1,0:T(4,128)} %copy-done.22) | copy-start | bytes 11524
  301.5 11.2 %all-to-all-start.4 = ((f32[16,1,4]{2,1,0:T(1,128)}), f32[16,1,4]{2,1,0:T(1,128)S(1)}, u32[]{:S(2)}, u32[]{:S(2)}) async-start(f32[16,1,4]{2,1,0:T(1,128)} %broadcast_in_dim.80), calls=%async_computation.4 | async-start | bytes 16384 | tf_op jit(solution)/shard_map/all_to_all | solution.py:12
  315.8 23.2 %all-to-all-start.5 = ((bf16[16,4,2560]{2,1,0:T(4,128)(2,1)}), bf16[16,4,2560]{2,1,0:T(4,128)(2,1)S(1)}, u32[]{:S(2)}, u32[]{:S(2)}) async-start(bf16[16,4,2560]{2,1,0:T(4,128)(2,1)} %broadcast_in_dim.81), calls=%async_computation.5 | async-start | bytes 655360 | tf_op jit(solution)/shard_map/all_to_all | solution.py:12
  339.2 9.0 %collective-permute-start = (bf16[4,2560]{1,0:T(4,128)(2,1)S(1)}, bf16[4,2560]{1,0:T(4,128)(2,1)S(1)}, u32[]{:S(2)}, u32[]{:S(2)}) collective-permute-start(bf16[4,2560]{1,0:T(4,128)(2,1)S(1)} %add_convert_fusion), channel_id=1, source_target_pairs={{0,1},{1,2},{2,3},{4,5},{5,6},{6,7},{8,9},{9,10},{10,11},{12,13},{... | collective-permute-start | bytes 61448 | tf_op jit(solution)/shard_map/ppermute | solution.py:39
  386.8 9.0 %collective-permute-start.1 = (bf16[4,2560]{1,0:T(4,128)(2,1)S(1)}, bf16[4,2560]{1,0:T(4,128)(2,1)S(1)}, u32[]{:S(2)}, u32[]{:S(2)}) collective-permute-start(bf16[4,2560]{1,0:T(4,128)(2,1)S(1)} %fusion.80), channel_id=1, source_target_pairs={{0,1},{1,2},{2,3},{4,5},{5,6},{6,7},{8,9},{9,10},{10,11},{12,13},{... | collective-permute-start | bytes 61448 | tf_op jit(solution)/shard_map/ppermute | solution.py:39
  429.7 9.0 %collective-permute-start.2 = (bf16[4,2560]{1,0:T(4,128)(2,1)S(1)}, bf16[4,2560]{1,0:T(4,128)(2,1)S(1)}, u32[]{:S(2)}, u32[]{:S(2)}) collective-permute-start(bf16[4,2560]{1,0:T(4,128)(2,1)S(1)} %fusion.84), channel_id=1, source_target_pairs={{0,1},{1,2},{2,3},{4,5},{5,6},{6,7},{8,9},{9,10},{10,11},{12,13},{... | collective-permute-start | bytes 61448 | tf_op jit(solution)/shard_map/ppermute | solution.py:39
  460.7 13.5 %all-to-all-start.11 = ((bf16[16,4,2560]{2,1,0:T(4,128)(2,1)}), bf16[16,4,2560]{2,1,0:T(4,128)(2,1)S(1)}, u32[]{:S(2)}, u32[]{:S(2)}) async-start(bf16[16,4,2560]{2,1,0:T(4,128)(2,1)} %broadcast_in_dim.87), calls=%async_computation.11 | async-start | bytes 655360 | tf_op jit(solution)/shard_map/all_to_all | solution.py:12
  474.3 9.1 %collective-permute-start.3 = (bf16[4,2560]{1,0:T(4,128)(2,1)S(1)}, bf16[4,2560]{1,0:T(4,128)(2,1)S(1)}, u32[]{:S(2)}, u32[]{:S(2)}) collective-permute-start(bf16[4,2560]{1,0:T(4,128)(2,1)S(1)} %fusion.88), channel_id=1, source_target_pairs={{0,1},{1,2},{2,3},{4,5},{5,6},{6,7},{8,9},{9,10},{10,11},{12,13},{... | collective-permute-start | bytes 61448 | tf_op jit(solution)/shard_map/ppermute | solution.py:39
  490.3 18.6 %copy-start.51 = (pred[4]{0:T(512)(128)(4,1)S(1)}, pred[4]{0:T(512)(128)(4,1)}, u32[]{:S(2)}) copy-start(pred[4]{0:T(512)(128)(4,1)} %get-tuple-element.96) | copy-start | bytes 16
  490.3 18.6 %copy-start.57 = (f32[4,5]{1,0:T(4,128)S(1)}, f32[4,5]{1,0:T(4,128)}, u32[]{:S(2)}) copy-start(f32[4,5]{1,0:T(4,128)} %copy-done.56) | copy-start | bytes 244
  491.0 11.2 %all-to-all-start.12 = ((f32[16,1,4]{2,1,0:T(1,128)}), f32[16,1,4]{2,1,0:T(1,128)S(1)}, u32[]{:S(2)}, u32[]{:S(2)}) async-start(f32[16,1,4]{2,1,0:T(1,128)} %broadcast_in_dim.88), calls=%async_computation.12 | async-start | bytes 16384 | tf_op jit(solution)/shard_map/all_to_all | solution.py:12
  505.2 13.6 %all-to-all-start.13 = ((bf16[16,4,2560]{2,1,0:T(4,128)(2,1)}), bf16[16,4,2560]{2,1,0:T(4,128)(2,1)S(1)}, u32[]{:S(2)}, u32[]{:S(2)}) async-start(bf16[16,4,2560]{2,1,0:T(4,128)(2,1)} %broadcast_in_dim.89), calls=%async_computation.13 | async-start | bytes 655360 | tf_op jit(solution)/shard_map/all_to_all | solution.py:12
  519.0 9.1 %collective-permute-start.4 = (bf16[4,2560]{1,0:T(4,128)(2,1)S(1)}, bf16[4,2560]{1,0:T(4,128)(2,1)S(1)}, u32[]{:S(2)}, u32[]{:S(2)}) collective-permute-start(bf16[4,2560]{1,0:T(4,128)(2,1)S(1)} %fusion.92), channel_id=1, source_target_pairs={{0,1},{1,2},{2,3},{4,5},{5,6},{6,7},{8,9},{9,10},{10,11},{12,13},{... | collective-permute-start | bytes 61448 | tf_op jit(solution)/shard_map/ppermute | solution.py:39
  535.6 11.2 %all-to-all-start.14 = ((f32[16,1,4]{2,1,0:T(1,128)}), f32[16,1,4]{2,1,0:T(1,128)S(1)}, u32[]{:S(2)}, u32[]{:S(2)}) async-start(f32[16,1,4]{2,1,0:T(1,128)} %broadcast_in_dim.90), calls=%async_computation.14 | async-start | bytes 16384 | tf_op jit(solution)/shard_map/all_to_all | solution.py:12
  549.9 13.5 %all-to-all-start.15 = ((bf16[16,4,2560]{2,1,0:T(4,128)(2,1)}), bf16[16,4,2560]{2,1,0:T(4,128)(2,1)S(1)}, u32[]{:S(2)}, u32[]{:S(2)}) async-start(bf16[16,4,2560]{2,1,0:T(4,128)(2,1)} %broadcast_in_dim.91), calls=%async_computation.15 | async-start | bytes 655360 | tf_op jit(solution)/shard_map/all_to_all | solution.py:12
  563.5 9.0 %collective-permute-start.5 = (bf16[4,2560]{1,0:T(4,128)(2,1)S(1)}, bf16[4,2560]{1,0:T(4,128)(2,1)S(1)}, u32[]{:S(2)}, u32[]{:S(2)}) collective-permute-start(bf16[4,2560]{1,0:T(4,128)(2,1)S(1)} %fusion.96), channel_id=1, source_target_pairs={{0,1},{1,2},{2,3},{4,5},{5,6},{6,7},{8,9},{9,10},{10,11},{12,13},{... | collective-permute-start | bytes 61448 | tf_op jit(solution)/shard_map/ppermute | solution.py:39
  581.5 13.7 %all-to-all-start.16 = ((f32[16,1,4]{2,1,0:T(1,128)}), f32[16,1,4]{2,1,0:T(1,128)S(1)}, u32[]{:S(2)}, u32[]{:S(2)}) async-start(f32[16,1,4]{2,1,0:T(1,128)} %broadcast_in_dim.93), calls=%async_computation.16 | async-start | bytes 16384 | tf_op jit(solution)/shard_map/all_to_all | solution.py:12
  598.3 13.5 %all-to-all-start.17 = ((bf16[16,4,2560]{2,1,0:T(4,128)(2,1)}), bf16[16,4,2560]{2,1,0:T(4,128)(2,1)S(1)}, u32[]{:S(2)}, u32[]{:S(2)}) async-start(bf16[16,4,2560]{2,1,0:T(4,128)(2,1)} %broadcast_in_dim.94), calls=%async_computation.17 | async-start | bytes 655360 | tf_op jit(solution)/shard_map/all_to_all | solution.py:12
  (63 other events, 432.2 us)
